TPU v7x, 128 devices: a whole 4x4x4 slice. The times are simulated.
128 devices in a mesh: tm: 4 (over y_hi, core), bank: 16 (over x, z), cuts: 2 (over y_lo).
Axes of the slice: x: 4, y: 4 (y_hi: 2, y_lo: 2; y = y_hi * 2 + y_lo), z: 4, core: 2. Of those that a mesh axis runs over, the one named last changes fastest.
Arguments:
- strain: float32 [2, 8192], P(None, 'tm'), may hold values from -6 to 6
- injections: float32 [8, 2, 512], replicated, may hold values from -12 to 12
- offsets: int32 [8, 2], replicated, may hold values from 0 to 7680
- slot_of: int32 [8192], replicated, may hold values from 0 to 8191, each once
- basis_filters: bfloat16 [16, 8, 256, 128], P('bank', 'cuts'), may hold values from -0.375 to 0.375
- recon_matrix: bfloat16 [16, 8, 128, 1024], P('bank', 'cuts'), may hold values from -0.1875 to 0.1875
Outputs:
- snr: bfloat16 [2, 8192, 2, 8192], P(None, ('tm', 'bank', 'cuts'))
All inputs are finite; a program needn't handle non-finite values.
Results may differ from a plain program's by a relative error of at most 0.0057.
Values may be sent and summed in bfloat16 or wider, within the bound.
A program may use at most 128 MiB of HBM per device.

v0:
```python
import jax
import jax.numpy as jnp
from jax import lax
from jax.sharding import PartitionSpec as P


def passed_along(block, axis, distance):
    devices = range(lax.axis_size(axis))
    route = [(i - distance, i) for i in devices if i - distance in devices]
    return lax.ppermute(block, axis, route)


def per_device(strain, injections, offsets, slot_of, basis_filters, recon_matrix):
    span_len = strain.shape[1]
    detectors = strain.shape[0]
    bank_count = lax.axis_size("bank")
    groups = lax.axis_size("cuts")
    per_group = basis_filters.shape[1]
    tap_count = basis_filters.shape[2]
    columns = recon_matrix.shape[3]
    history_len = per_group * groups * tap_count
    wave_len = injections.shape[2]
    anchor = lax.axis_index("tm") * span_len
    where_at = offsets[:, :, None] + jnp.arange(wave_len, dtype=jnp.int32)[None, None, :] - anchor
    inside = (where_at >= 0) & (where_at < span_len)
    where_at = jnp.where(inside, where_at, span_len)
    detector = jnp.broadcast_to(
        jnp.arange(detectors, dtype=jnp.int32)[None, :, None], where_at.shape
    )
    injected = strain.at[detector, where_at].add(injections, mode="drop")
    samples = injected.astype(jnp.bfloat16)
    earlier = passed_along(samples, "tm", 1)
    extended = jnp.concatenate([earlier, samples], axis=1)
    first_slice = lax.axis_index("cuts") * per_group
    outputs = []
    for local_slice in range(per_group):
        start_at = history_len - (first_slice + local_slice) * tap_count - (tap_count - 1)
        window = lax.dynamic_slice_in_dim(extended, start_at, span_len + tap_count - 1, 1)
        kernel = basis_filters[0, local_slice][::-1][:, None, :]
        basis_out = lax.conv_general_dilated(
            window[:, :, None],
            kernel,
            (1,),
            "VALID",
            dimension_numbers=("NWC", "WIO", "NWC"),
            preferred_element_type=jnp.float32,
        )
        outputs.append(basis_out.astype(jnp.bfloat16))
    block_len = span_len // (bank_count * groups)
    partial_sum = jnp.zeros((detectors, span_len, columns), jnp.float32)
    for local_slice in range(per_group):
        partial_sum = partial_sum + jnp.einsum(
            "dtm,mc->dtc",
            outputs[local_slice],
            recon_matrix[0, local_slice],
            preferred_element_type=jnp.float32,
        )
    shaped = partial_sum.reshape(detectors, bank_count, groups, block_len, columns)
    summed = lax.psum_scatter(shaped, "cuts", scatter_dimension=2, tiled=True)
    slot_snr = summed.astype(jnp.bfloat16)
    regrouped = lax.all_to_all(slot_snr, "bank", split_axis=1, concat_axis=1, tiled=True)
    per_bank = columns // 2
    ordered = (
        regrouped.reshape(detectors, bank_count, block_len, 2, per_bank)
        .transpose(0, 2, 3, 1, 4)
        .reshape(detectors, block_len, 2, bank_count * per_bank)
    )
    return jnp.take(ordered, slot_of, axis=3)


def solution(mesh):
    return jax.shard_map(
        per_device,
        mesh=mesh,
        in_specs=(
            P(None, "tm"),
            P(),
            P(),
            P(),
            P("bank", "cuts", None, None),
            P("bank", "cuts", None, None),
        ),
        out_specs=P(None, ("tm", "bank", "cuts"), None, None),
        check_vma=False,
    )
```

profile of v0, /device:TPU:108, one launch (start us, length us, event | category | flops | bytes accessed | tf_op | source)
XLA Modules:
  0.0 797.7 jit_solution(17580326479116514093)
XLA Ops:
  0.0 0.8 compare_select_fusion
  0.8 0.7 multiply_reduce_fusion
  1.5 0.7 and_reduce_fusion
  2.3 0.8 copy.104
  3.1 0.7 copy.102
  3.8 48.8 %scatter_fusion = f32[4096]{0:T(1024)S(1)} fusion(f32[4096]{0:T(1024)S(1)} %bitcast.95, s32[8192]{0:T(1024)S(1)} %bitcast.103, f32[8192]{0:T(1024)S(1)} %bitcast.104), kind=kCustom, calls=%fused_computation.1 | custom fusion | flops 8192 | bytes 131072
  52.6 1.3 collective-permute-start
  54.2 0.7 rev.14
  54.9 0.7 rev.15
  55.5 0.6 dynamic-slice
  56.2 0.7 dynamic-slice_bitcast_fusion
  57.3 15.6 %select_convert_fusion.2 = bf16[16,288,128]{2,0,1:T(8,128)(2,1)S(1)} fusion(bf16[16,543,1]{0,2,1:T(2,128)(2,1)S(1)} %copy.82, pred[16,288]{0,1:T(8,128)(4,1)S(1)} %bitcast.112, bf16[256,1,128]{2,0,1:T(8,128)(2,1)S(1)} %bitcast.109), kind=kOutput, calls=%fused_computation.8 | convolution fusion | flops 303169536 | bytes 1267168 | tf_op jit(solution)/shard_map/conv_general_dilated | solution.py:40
  72.9 0.3 copy.84
  73.7 15.9 %select_convert_fusion.3 = bf16[16,288,128]{2,0,1:T(8,128)(2,1)S(1)} fusion(bf16[16,543,1]{0,2,1:T(2,128)(2,1)S(1)} %copy.79, pred[16,288]{0,1:T(8,128)(4,1)S(1)} %bitcast.113, bf16[256,1,128]{2,0,1:T(8,128)(2,1)S(1)} %bitcast.108), kind=kOutput, calls=%fused_computation.9 | convolution fusion | flops 303169536 | bytes 1267168 | tf_op jit(solution)/shard_map/conv_general_dilated | solution.py:40
  89.6 0.3 copy.81
  89.9 8.0 %fusion.4 = f32[2,2048,1024]{2,1,0:T(8,128)} fusion(bf16[2,2304,128]{2,1,0:T(8,128)(2,1)S(1)} %bitcast.100, bf16[1,4,128,1024]{3,2,1,0:T(8,128)(2,1)S(1)} %copy-done), kind=kOutput, calls=%fused_computation.13 | convolution fusion | flops 1073741824 | bytes 18087936 | tf_op jit(solution)/shard_map/dtm,mc->dtc/dot_general | solution.py:52
  98.0 8.1 %fusion.6 = f32[2,2048,1024]{2,1,0:T(8,128)} fusion(bf16[2,2304,128]{2,1,0:T(8,128)(2,1)S(1)} %bitcast.101, bf16[1,4,128,1024]{3,2,1,0:T(8,128)(2,1)S(1)} %copy-done), kind=kOutput, calls=%fused_computation.15 | convolution fusion | flops 1073741824 | bytes 18087936 | tf_op jit(solution)/shard_map/dtm,mc->dtc/dot_general | solution.py:52
  106.5 15.8 %select_convert_fusion.1 = bf16[16,288,128]{2,0,1:T(8,128)(2,1)S(1)} fusion(bf16[16,543,1]{0,2,1:T(2,128)(2,1)S(1)} %copy.85, pred[16,288]{0,1:T(8,128)(4,1)S(1)} %bitcast.114, bf16[256,1,128]{2,0,1:T(8,128)(2,1)S(1)} %bitcast.107), kind=kOutput, calls=%fused_computation.7 | convolution fusion | flops 303169536 | bytes 1267168 | tf_op jit(solution)/shard_map/conv_general_dilated | solution.py:40
  122.3 0.3 copy.87
  122.6 8.0 %fusion.2 = f32[2,2048,1024]{2,1,0:T(8,128)} fusion(bf16[2,2304,128]{2,1,0:T(8,128)(2,1)S(1)} %bitcast.102, bf16[1,4,128,1024]{3,2,1,0:T(8,128)(2,1)S(1)} %copy-done), kind=kOutput, calls=%fused_computation.11 | convolution fusion | flops 1073741824 | bytes 18087936 | tf_op jit(solution)/shard_map/dtm,mc->dtc/dot_general | solution.py:52
  131.1 15.6 %select_convert_fusion = bf16[16,288,128]{2,0,1:T(8,128)(2,1)S(1)} fusion(bf16[16,543,1]{0,2,1:T(2,128)(2,1)S(1)} %copy.88, pred[16,288]{0,1:T(8,128)(4,1)S(1)} %bitcast.115, bf16[256,1,128]{2,0,1:T(8,128)(2,1)S(1)} %bitcast.106), kind=kOutput, calls=%fused_computation.6 | convolution fusion | flops 303169536 | bytes 1267168 | tf_op jit(solution)/shard_map/conv_general_dilated | solution.py:40
  147.0 22.9 %add_add_fusion = f32[2,2048,1024]{2,1,0:T(8,128)} fusion(f32[2,2048,1024]{2,1,0:T(8,128)} %fusion.2, f32[2,2048,1024]{2,1,0:T(8,128)} %fusion.6, f32[2,2048,1024]{2,1,0:T(8,128)} %fusion.4, bf16[2,2304,128]{2,1,0:T(8,128)(2,1)S(1)} %bitcast.99, bf16[1,4,128,1024]{3,2,1,0:T(8,128)(2,1)S(1)} %copy-done), kind=kOutput, calls=%fused_computation.2 | convolution fusion | flops 1086324736 | bytes 68419584 | tf_op jit(solution)/shard_map/dtm,mc->dtc/dot_general | solution.py:52
  169.9 11.8 %copy.91 = f32[2,16,2,64,1024]{4,3,0,2,1:T(8,128)} copy(f32[2,16,2,64,1024]{4,3,2,1,0:T(8,128)} %bitcast.96) | data formatting | bytes 33554432 | tf_op jit(solution)/shard_map/reshape | solution.py:58
  181.7 384.4 %all-reduce.2 = bf16[2,16,2,64,1024]{4,3,0,2,1:T(8,128)(2,1)} all-reduce(f32[2,16,2,64,1024]{4,3,0,2,1:T(8,128)} %copy.91), channel_id=2, replica_groups=mesh['tm'=4,'bank'=16,'cuts'=2] {'cuts'}, use_global_device_ids=true, to_apply=%region_1.2.clone | all-reduce | flops 4194304 | bytes 25165824
  566.2 5.6 dynamic-slice_convert_fusion
  571.7 7.1 all-to-all-start
  578.8 67.0 %all-to-all-done = bf16[2,16,1,64,1024]{4,3,0,2,1:T(8,128)(2,1)} async-done(((bf16[2,16,1,64,1024]{4,3,0,2,1:T(8,128)(2,1)}), bf16[2,16,1,64,1024]{4,3,0,2,1:T(8,128)(2,1)}, u32[]{:S(2)}, u32[]{:S(2)}) %all-to-all-start) | async-done | bytes 4194336 | tf_op jit(solution)/shard_map/all_to_all | solution.py:61
  645.9 7.8 reshape.112
  653.7 21.6 %copy.98 = bf16[2,64,2,16,512]{1,2,4,3,0:T(2,128)(2,1)} copy(bf16[2,64,2,16,512]{4,2,1,0,3:T(2,128)(2,1)} %bitcast.98) | data formatting | bytes 8388608 | tf_op jit(solution)/shard_map/reshape | solution.py:66
  675.3 69.9 %gather_fusion = bf16[8192,2,64,2]{2,3,1,0:T(2,128)(2,1)} fusion(bf16[2,64,2,8192]{1,2,3,0:T(2,128)(2,1)} %bitcast.97, s32[8192]{0:T(1024)S(1)} %fusion.27), kind=kCustom, calls=%fused_computation | custom fusion | bytes 8421376 | tf_op jit(solution)/shard_map/jit(_take)/gather | solution.py:68
  745.2 31.2 %fusion = bf16[2,64,2,8192]{1,2,0,3:T(2,128)(2,1)} fusion(bf16[8192,2,64,2]{2,3,1,0:T(2,128)(2,1)} %gather_fusion, pred[8192]{0:T(1024)(128)(4,1)S(1)} %compare_and_fusion), kind=kLoop, calls=%fused_computation.5 | loop fusion | flops 2097152 | bytes 8396800 | tf_op jit(solution)/shard_map/jit(_take)/select_n | solution.py:68
  776.4 21.1 %copy.95 = bf16[2,64,2,8192]{3,2,1,0:T(2,128)(2,1)} copy(bf16[2,64,2,8192]{1,2,0,3:T(2,128)(2,1)} %fusion) | data formatting | bytes 8388608 | tf_op jit(solution)/shard_map/jit(_take)/select_n | solution.py:68
  (53 shorter events, 2.3 us)
Async XLA Ops:
  3.8 50.1 %copy-start.1 = (bf16[1,4,256,128]{3,2,1,0:T(8,128)(2,1)S(1)}, bf16[1,4,256,128]{3,2,1,0:T(8,128)(2,1)}, u32[]{:S(2)}) copy-start(bf16[1,4,256,128]{3,2,1,0:T(8,128)(2,1)} %param.10) | copy-start | bytes 786436
  3.8 51.7 %copy-start.8 = (u32[128]{0:T(128)S(1)}, u32[128]{0:T(128)}, u32[]{:S(2)}) copy-start(u32[128]{0:T(128)} %constant.93) | copy-start | bytes 1540
  3.8 53.5 %copy-start.7 = (pred[16,288]{0,1:T(32,128)(4,1)S(1)}, pred[16,288]{0,1:T(32,128)(4,1)}, u32[]{:S(2)}) copy-start(pred[16,288]{0,1:T(32,128)(4,1)} %constant.86) | copy-start | bytes 13828
  52.6 3.5 collective-permute-start
  73.7 16.3 %copy-start = (bf16[1,4,128,1024]{3,2,1,0:T(8,128)(2,1)S(1)}, bf16[1,4,128,1024]{3,2,1,0:T(8,128)(2,1)}, u32[]{:S(2)}) copy-start(bf16[1,4,128,1024]{3,2,1,0:T(8,128)(2,1)} %param.11) | copy-start | bytes 3145732
  98.0 8.1 %copy-start.6 = (bf16[2,2303,1]{1,0,2:T(2,128)(2,1)S(1)}, bf16[2,2303,1]{1,0,2:T(2,128)(2,1)}, u32[]{:S(2)}) copy-start(bf16[2,2303,1]{1,0,2:T(2,128)(2,1)} %get-tuple-element.10) | copy-start | bytes 27640
  98.0 8.5 %copy-start.4 = (bf16[256,128]{1,0:T(8,128)(2,1)S(1)}, bf16[256,128]{1,0:T(8,128)(2,1)}, u32[]{:S(2)}) copy-start(bf16[256,128]{1,0:T(8,128)(2,1)} %rev.14) | copy-start | bytes 196612
  122.6 8.1 %copy-start.5 = (bf16[2,2303,1]{1,0,2:T(2,128)(2,1)S(1)}, bf16[2,2303,1]{1,0,2:T(2,128)(2,1)}, u32[]{:S(2)}) copy-start(bf16[2,2303,1]{1,0,2:T(2,128)(2,1)} %get-tuple-element.9) | copy-start | bytes 27640
  122.6 8.5 %copy-start.3 = (bf16[256,128]{1,0:T(8,128)(2,1)S(1)}, bf16[256,128]{1,0:T(8,128)(2,1)}, u32[]{:S(2)}) copy-start(bf16[256,128]{1,0:T(8,128)(2,1)} %rev.15) | copy-start | bytes 196612
  571.7 7.1 copy-start.2
  571.7 74.1 %all-to-all-start = ((bf16[2,16,1,64,1024]{4,3,0,2,1:T(8,128)(2,1)}), bf16[2,16,1,64,1024]{4,3,0,2,1:T(8,128)(2,1)}, u32[]{:S(2)}, u32[]{:S(2)}) async-start(bf16[2,16,1,64,1024]{4,3,0,2,1:T(8,128)(2,1)} %dynamic-slice_convert_fusion), calls=%async_computation | async-start | bytes 8388608 | tf_op jit(solution)/shard_map/all_to_all | solution.py:61
where the time goes:
time: 809 us; the launch traced here: 798 us
  blocking collectives  384 us (47%)
  local copies, waits for them, and re-layouts  145 us (18%)
  matrix products  110 us (14%)
  other arithmetic  82.6 us (10%)
  waiting for transfers between devices  67 us (8%)
  starting transfers between devices  8.35 us (1%)
    unnamed x1, blocking collectives  384 us
    gather x1, local copies, waits for them, and re-layouts, per_device(): return jnp.take(ordered, slot_of, axis=3)  69.9 us
    all_to_all x1, waiting for transfers between devices, per_device(): lax.all_to_all(slot_snr, 'bank', split_axis=1, concat_axis=1, tiled=True)  67 us
    conv_general_dilated x4, matrix products, per_device(): lax.conv_general_dilated(window[:, :, None], kernel, (1,), 'VALID', dimen...  62.9 us
    unnamed x4, other arithmetic  50.2 us
    dot_general x4, matrix products, per_device(): jnp.einsum('dtm,mc->dtc', outputs[local_slice], recon_matrix[0, local_sli...  47 us
    select_n x1, other arithmetic, per_device(): return jnp.take(ordered, slot_of, axis=3)  31.2 us
    reshape x1, local copies, waits for them, and re-layouts, per_device(): ordered = regrouped.reshape(detectors, bank_count, block_len, 2, per_bank...  21.6 us
  transfers between devices with their start and end apart: 2, of which 1 were waited for; matrix products, arithmetic and copies ran while one was open for 0% of the time, Pallas kernels for 0%

commit v1 on v0

v1 whole, which is shorter than its diff:
```python
import functools

import jax
import jax.numpy as jnp
from jax import lax
from jax.experimental import pallas as pl
from jax.experimental.pallas import tpu as pltpu
from jax.sharding import PartitionSpec as P

MESH = pl.DeviceIdType.MESH
LANES = 128
BLOCK = 64
PIECES = 4
ORDER = (
    (1, 1), (3, 3), (1, 3), (3, 1),
    (1, 0), (3, 0), (0, 1), (0, 3),
    (2, 2), (2, 0), (0, 2),
    (2, 1), (2, 3), (1, 2), (3, 2),
)


def pair_select(dtype):
    row = lax.broadcasted_iota(jnp.int32, (256, 256), 0)
    col = lax.broadcasted_iota(jnp.int32, (256, 256), 1)
    return ((row // 2 == col % LANES) & (row % 2 == col // LANES)).astype(dtype)


def inject_kernel(offsets, strain, injections, out, acc):
    detectors, rows = strain.shape[0], strain.shape[1]
    anchor = lax.axis_index("tm") * (rows * LANES)
    acc[...] = jnp.zeros_like(acc)
    lane = lax.broadcasted_iota(jnp.int32, (8, LANES), 1)
    zeros = jnp.zeros((4, LANES), jnp.float32)
    for d in range(detectors):
        acc[d, pl.ds(8, rows), :] = strain[d]
        for i in range(injections.shape[0]):
            first = offsets[i, d] - anchor
            row = first // LANES
            shift = first - row * LANES
            wave = jnp.concatenate([injections[i, d], zeros], axis=0)
            rolled = pltpu.roll(wave, shift, axis=1)
            placed = jnp.where(lane >= shift, rolled, pltpu.roll(rolled, 1, axis=0))
            where = jnp.clip(row, -8, rows) + 8
            acc[d, pl.ds(where, 8), :] += placed
        out[d] = acc[d, pl.ds(8, rows), :].astype(jnp.bfloat16).astype(jnp.float32)


def inject(strain, injections, offsets):
    detectors, span = strain.shape
    rows = span // LANES
    shaped = strain.reshape(detectors, rows, LANES)
    waves = injections.reshape(*injections.shape[:2], -1, LANES)
    return pl.pallas_call(
        inject_kernel,
        out_shape=jax.ShapeDtypeStruct(shaped.shape, jnp.float32),
        in_specs=[
            pl.BlockSpec(memory_space=pltpu.SMEM),
            pl.BlockSpec(memory_space=pltpu.VMEM),
            pl.BlockSpec(memory_space=pltpu.VMEM),
        ],
        out_specs=pl.BlockSpec(memory_space=pltpu.VMEM),
        scratch_shapes=[pltpu.VMEM((detectors, rows + 16, LANES), jnp.float32)],
    )(offsets, shaped, waves)


def filter_kernel(
    samples, filters, recon, out,
    spans, windows, history, taps, raw, weights, basis, staged,
    local_sem, halo_sem, send_sem, recv_sem, pass_sem, got_sem, out_sem, in_sem,
):
    tm, bank, cuts = lax.axis_index("tm"), lax.axis_index("bank"), lax.axis_index("cuts")
    hi, core = tm // 2, tm % 2
    x, z = bank // 4, bank % 4
    partner = {"tm": hi * 2 + 1 - core}
    beside = ({"cuts": 1 - cuts}, {"tm": (1 - hi) * 2 + core, "cuts": 1 - cuts})
    after, before = {"tm": (tm + 1) % 4}, {"tm": (tm + 3) % 4}

    barrier = pltpu.get_barrier_semaphore()
    for device in (*beside, after, before, *({"bank": (bank + k) % 16} for k in range(1, 16))):
        pl.semaphore_signal(barrier, inc=1, device_id=device, device_id_type=MESH)

    locals_ = [
        pltpu.make_async_copy(filters.at[0], taps.at[pl.ds(4 * cuts, 4)], local_sem.at[0]),
        pltpu.make_async_copy(recon.at[0], raw.at[pl.ds(4 * cuts, 4)], local_sem.at[1]),
        pltpu.make_async_copy(samples, spans.at[1], local_sem.at[2]),
    ]
    for copy in locals_:
        copy.start()
    pl.semaphore_wait(barrier, 19)

    halo = pltpu.make_async_remote_copy(
        samples, spans.at[0], halo_sem.at[0], halo_sem.at[1],
        device_id=after, device_id_type=MESH,
    )
    halo.start()
    sends = []
    for j in range(2):
        mine = 2 * core + j
        for n, (source, target) in enumerate(((filters, taps), (recon, raw))):
            sends.append(pltpu.make_async_remote_copy(
                source.at[0, mine], target.at[4 * cuts + mine],
                send_sem.at[j, n], recv_sem.at[j, n],
                device_id=beside[j], device_id_type=MESH,
            ))
            sends[-1].start()

    locals_[2].wait()
    halo.wait()

    lane = lax.broadcasted_iota(jnp.int32, (32, LANES), 1)
    low = lane < BLOCK
    row32 = lax.broadcasted_iota(jnp.int32, (32, LANES), 0)
    known = (row32 >= 16) | (tm > 0)
    for d in range(2):
        line = jnp.concatenate([spans[0, d], spans[1, d]], axis=0)
        line = jnp.where(known, line, 0.0)
        swapped = pltpu.roll(line, BLOCK, axis=1)
        if d == 1:
            windows[0] = line
            windows[1] = jnp.where(low, swapped, pltpu.roll(swapped, 31, axis=0))
        else:
            windows[2] = swapped
            windows[3] = jnp.where(low, pltpu.roll(line, 31, axis=0), line)
    half = lax.broadcasted_iota(jnp.int32, (BLOCK, LANES), 1) < BLOCK

    def fill(j, carry):
        for odd in range(2):
            row = j if odd else j + cuts
            tile = 60 + cuts - 2 * j if odd else 61 - cuts - 2 * j
            parts = []
            for kind in (2 + odd, odd):
                wide = jnp.broadcast_to(windows[kind, pl.ds(row, 1), :], (BLOCK, LANES))
                parts.append(pltpu.roll(wide, 0, axis=1, stride=1, stride_axis=0))
            value = jnp.where(half, parts[0], parts[1]).astype(jnp.bfloat16)
            history[pl.ds(pl.multiple_of(tile * BLOCK, BLOCK), BLOCK), :] = value
        return carry

    lax.fori_loop(0, 31, fill, 0)

    select = pair_select(jnp.bfloat16)

    def turn(slot):
        for h in range(4):
            pair = jnp.concatenate(
                [raw[slot, :, pl.ds(128 * h, 128)], raw[slot, :, pl.ds(512 + 128 * h, 128)]],
                axis=1,
            )
            turned = lax.dot_general(
                select, pair, (((1,), (1,)), ((), ())), preferred_element_type=jnp.float32
            )
            weights[slot, pl.ds(256 * h, 256), :] = turned.astype(jnp.bfloat16)

    locals_[0].wait()
    locals_[1].wait()
    for i in range(4):
        turn(4 * cuts + i)
    other = 4 * (1 - cuts)
    passes = []
    for n, target in enumerate((taps, raw)):
        for j in range(2):
            sends[2 * j + n].wait_recv()
            held = target.at[other + 2 * core + j]
            passes.append(pltpu.make_async_remote_copy(
                held, held, pass_sem.at[j, n], got_sem.at[j, n],
                device_id=partner, device_id_type=MESH,
            ))
            passes[-1].start()
    for j in range(2):
        turn(other + 2 * core + j)
    for copy in passes:
        copy.wait_recv()
    for j in range(2):
        turn(other + 2 * (1 - core) + j)

    def target_of(k):
        dx, dz = 0, 0
        for i, (a, b) in enumerate(ORDER):
            dx = jnp.where(k == i, a, dx)
            dz = jnp.where(k == i, b, dz)
        return ((x + dx) % 4) * 4 + (z + dz) % 4

    rows = weights.shape[1] // PIECES

    def piece(k, p, h):
        part = pl.ds(h * rows, rows)
        return pltpu.make_async_remote_copy(
            staged.at[k, part], out.at[bank, part], out_sem.at[k, h], in_sem.at[k, h],
            device_id={"bank": p}, device_id_type=MESH,
        )

    def block(k, carry):
        p = target_of(k)
        for s in range(8):
            start = pl.multiple_of(LANES * (15 - p) + 256 * s, LANES)
            made = lax.dot_general(
                taps[s], history[pl.ds(start, 256), :], (((0,), (0,)), ((), ())),
                preferred_element_type=jnp.float32,
            )
            basis[pl.ds(LANES * s, LANES), :] = made.astype(jnp.bfloat16)
        for h in range(PIECES):
            total = jnp.zeros((rows, LANES), jnp.float32)
            for s in range(8):
                total += jnp.dot(
                    weights[s, pl.ds(h * rows, rows), :], basis[pl.ds(LANES * s, LANES), :],
                    preferred_element_type=jnp.float32,
                )
            staged[k, pl.ds(h * rows, rows), :] = total.astype(jnp.bfloat16)

            @pl.when(k < 15)
            def _():
                piece(k, p, h).start()
        return carry

    lax.fori_loop(0, 16, block, 0)
    own = pltpu.make_async_copy(staged.at[15], out.at[bank], local_sem.at[0])
    own.start()

    def finish(k, carry):
        for h in range(PIECES):
            copy = piece(k, target_of(k), h)
            copy.wait_send()
            copy.wait_recv()
        return carry

    lax.fori_loop(0, 15, finish, 0)
    own.wait()
    for copy in (*sends, *passes):
        copy.wait_send()


def filter_and_exchange(samples, filters, recon):
    any_space = pl.BlockSpec(memory_space=pl.ANY)
    columns = recon.shape[3]
    dma = pltpu.SemaphoreType.DMA
    return pl.pallas_call(
        filter_kernel,
        out_shape=jax.ShapeDtypeStruct((16, columns, LANES), jnp.bfloat16),
        in_specs=[any_space] * 3,
        out_specs=any_space,
        scratch_shapes=[
            pltpu.VMEM((2, 2, 16, LANES), jnp.float32),
            pltpu.VMEM((4, 32, LANES), jnp.float32),
            pltpu.VMEM((62 * BLOCK, LANES), jnp.bfloat16),
            pltpu.VMEM((8, 256, 128), jnp.bfloat16),
            pltpu.VMEM((8, 128, columns), jnp.bfloat16),
            pltpu.VMEM((8, columns, 128), jnp.bfloat16),
            pltpu.VMEM((1024, LANES), jnp.bfloat16),
            pltpu.VMEM((16, columns, LANES), jnp.bfloat16),
            dma((3,)), dma((2,)), dma((2, 2)), dma((2, 2)), dma((2, 2)), dma((2, 2)),
            dma((15, PIECES)), dma((15, PIECES)),
        ],
        compiler_params=pltpu.CompilerParams(
            collective_id=0, has_side_effects=True, vmem_limit_bytes=40 * 2**20
        ),
    )(samples, filters, recon)


def order_kernel(width, slots, pairs, out, picked):
    base = pl.program_id(0) * width

    def pick(i, carry):
        for u in range(16):
            picked[i * 16 + u] = pairs[slots[base + i * 16 + u]]
        return carry

    lax.fori_loop(0, width // 16, pick, 0)
    select = pair_select(jnp.bfloat16)
    for j in range(width // 256):
        turned = []
        for h in range(2):
            rows = picked.at[pl.ds(j * 256 + h * 128, 128)].reshape(256, LANES)[...]
            turned.append(lax.dot_general(
                rows, select, (((0,), (0,)), ((), ())), preferred_element_type=jnp.float32
            ).astype(jnp.bfloat16))
        stacked = jnp.concatenate(
            [jnp.concatenate([t[:, q * 128:(q + 1) * 128] for t in turned], axis=1) for q in range(2)],
            axis=0,
        )
        mixed = jnp.dot(select, stacked, preferred_element_type=jnp.float32).astype(jnp.bfloat16)
        out[:, :, :, pl.ds(j * 256, 256)] = mixed.reshape(2, BLOCK, 2, 256)


def put_in_order(slot_of, arrived):
    count = slot_of.shape[0]
    width = 1024
    return pl.pallas_call(
        functools.partial(order_kernel, width),
        out_shape=jax.ShapeDtypeStruct((2, BLOCK, 2, count), jnp.bfloat16),
        grid_spec=pltpu.PrefetchScalarGridSpec(
            num_scalar_prefetch=1,
            grid=(count // width,),
            in_specs=[pl.BlockSpec((count, 2, LANES), lambda i, s: (0, 0, 0))],
            out_specs=pl.BlockSpec((2, BLOCK, 2, width), lambda i, s: (0, 0, 0, i)),
            scratch_shapes=[pltpu.VMEM((width, 2, LANES), jnp.bfloat16)],
        ),
        compiler_params=pltpu.CompilerParams(vmem_limit_bytes=40 * 2**20),
    )(slot_of, arrived.reshape(count, 2, LANES))


def per_device(strain, injections, offsets, slot_of, basis_filters, recon_matrix):
    samples = inject(strain, injections, offsets)
    arrived = filter_and_exchange(samples, basis_filters, recon_matrix)
    return put_in_order(slot_of, arrived)


def solution(mesh):
    return jax.shard_map(
        per_device,
        mesh=mesh,
        in_specs=(
            P(None, "tm"), P(), P(), P(),
            P("bank", "cuts", None, None), P("bank", "cuts", None, None),
        ),
        out_specs=P(None, ("tm", "bank", "cuts"), None, None),
        check_vma=False,
    )
```

time: 809 us -> 102 us (0.13)
  the two profiles are of different devices: /device:TPU:108 before, /device:TPU:1 now
where the time goes in v1:
time: 102 us
  Pallas kernels  94.7 us (93%)
  local copies, waits for them, and re-layouts  6.97 us (7%)
    pallas_call x1, Pallas kernels, filter_and_exchange(): pl.pallas_call(filter_kernel, out_shape=jax.ShapeDtypeStruct((16, columns...  76.3 us
    pallas_call x1, Pallas kernels, put_in_order(): pl.pallas_call(functools.partial(order_kernel, width), out_shape=jax.Shap...  16.9 us
    unnamed x10, local copies, waits for them, and re-layouts  5.56 us

profile of v1, /device:TPU:1, one launch (start us, length us, event | category | flops | bytes accessed | tf_op | source)
XLA Modules:
  0.0 101.7 jit_solution(12612032517202207969)
XLA Ops:
  0.0 0.0 copy-start.3
  0.0 1.4 %copy.7.offsets = s32[8,2]{1,0:T(8,128)} copy(s32[8,2]{0,1:T(2,128)} %param.8) | data formatting | bytes 128 | tf_op args[2]
  1.4 1.3 %copy.10 = f32[1,2,16,128]{3,2,1,0:T(8,128)} copy(f32[1,2,16,128]{3,1,2,0:T(2,128)} %bitcast.7) | data formatting | bytes 32768
  2.7 1.4 %reshape.10.injections = f32[8,2,4,128]{3,2,1,0:T(4,128)} reshape(f32[8,2,512]{2,1,0:T(2,128)} %param.7) | data formatting | bytes 65536 | tf_op jit(solution)/shard_map/reshape | solution.py:52
  4.1 1.6 %shard_map.64.samples = f32[2,16,128]{2,1,0:T(8,128)} custom-call(s32[8,2]{1,0:T(8,128)} %copy.7.offsets, f32[2,16,128]{2,1,0:T(8,128)} %bitcast.6, f32[8,2,4,128]{3,2,1,0:T(4,128)} %reshape.10.injections), custom_call_target="tpu_custom_call" | custom-call | tf_op jit(solution)/shard_map/pallas_call | solution.py:53
  5.7 0.0 copy-start
  5.7 1.2 %copy-done = bf16[1,4,128,1024]{3,2,1,0:T(8,128)(2,1)S(1)} copy-done((bf16[1,4,128,1024]{3,2,1,0:T(8,128)(2,1)S(1)}, bf16[1,4,128,1024]{3,2,1,0:T(8,128)(2,1)}, u32[]{:S(2)}) %copy-start) | copy-done | bytes 1048600
  6.9 0.0 copy-start.1
  6.9 0.9 copy-done.1
  7.8 0.0 copy-start.2
  7.8 0.7 copy-done.2
  8.5 76.3 %shard_map.65 = bf16[16,1024,128]{2,1,0:T(8,128)(2,1)S(1)} custom-call(f32[2,16,128]{2,1,0:T(8,128)S(1)} %copy-done.2, bf16[1,4,256,128]{3,2,1,0:T(8,128)(2,1)S(1)} %copy-done.1, bf16[1,4,128,1024]{3,2,1,0:T(8,128)(2,1)S(1)} %copy-done), custom_call_target="tpu_custom_call" | custom-call | tf_op jit(solution)/shard_map/pallas_call | solution.py:235
  84.9 0.0 copy-done.3
  84.9 16.9 %shard_map.66 = bf16[2,64,2,8192]{3,2,1,0:T(2,128)(2,1)} custom-call(s32[8192]{0:T(1024)S(1)} %copy-done.3, bf16[8192,2,128]{2,1,0:T(2,128)(2,1)S(1)} %bitcast.5), custom_call_target="tpu_custom_call" | custom-call | tf_op jit(solution)/shard_map/pallas_call | solution.py:286
Async XLA Ops:
  0.0 84.9 %copy-start.3 = (s32[8192]{0:T(1024)S(1)}, s32[8192]{0:T(1024)}, u32[]{:S(2)}) copy-start(s32[8192]{0:T(1024)} %slots.1) | copy-start | bytes 98308
  5.7 1.2 %copy-start = (bf16[1,4,128,1024]{3,2,1,0:T(8,128)(2,1)S(1)}, bf16[1,4,128,1024]{3,2,1,0:T(8,128)(2,1)}, u32[]{:S(2)}) copy-start(bf16[1,4,128,1024]{3,2,1,0:T(8,128)(2,1)} %recon.1) | copy-start | bytes 3145732
  6.9 0.9 copy-start.1
  7.8 0.7 copy-start.2

commit v2 on v1

v2 whole, which is shorter than its diff:
```python
import functools

import jax
import jax.numpy as jnp
from jax import lax
from jax.experimental import pallas as pl
from jax.experimental.pallas import tpu as pltpu
from jax.sharding import PartitionSpec as P

MESH = pl.DeviceIdType.MESH
LANES = 128
BLOCK = 64
PIECES = 4
ORDER = (
    (1, 1), (3, 3), (1, 3), (3, 1),
    (1, 0), (3, 0), (0, 1), (0, 3),
    (2, 2), (2, 0), (0, 2),
    (2, 1), (2, 3), (1, 2), (3, 2),
)


def pair_select(dtype):
    row = lax.broadcasted_iota(jnp.int32, (256, 256), 0)
    col = lax.broadcasted_iota(jnp.int32, (256, 256), 1)
    return ((row // 2 == col % LANES) & (row % 2 == col // LANES)).astype(dtype)


def filter_kernel(
    offsets, strain, injections, filters, recon, out,
    spans, waves, windows, history, taps, raw, weights, basis, staged,
    local_sem, halo_sem, send_sem, recv_sem, pass_sem, got_sem, out_sem, in_sem,
):
    tm, bank, cuts = lax.axis_index("tm"), lax.axis_index("bank"), lax.axis_index("cuts")
    hi, core = tm // 2, tm % 2
    x, z = bank // 4, bank % 4
    partner = {"tm": hi * 2 + 1 - core}
    beside = ({"cuts": 1 - cuts}, {"tm": (1 - hi) * 2 + core, "cuts": 1 - cuts})
    after, before = {"tm": (tm + 1) % 4}, {"tm": (tm + 3) % 4}
    other = 4 * (1 - cuts)

    barrier = pltpu.get_barrier_semaphore()
    for device in (*beside, after, before, *({"bank": (bank + k) % 16} for k in range(1, 16))):
        pl.semaphore_signal(barrier, inc=1, device_id=device, device_id_type=MESH)

    locals_ = [
        pltpu.make_async_copy(strain, spans.at[1], local_sem.at[0]),
        pltpu.make_async_copy(injections, waves, local_sem.at[1]),
        pltpu.make_async_copy(recon.at[0], raw.at[pl.ds(4 * cuts, 4)], local_sem.at[2]),
        pltpu.make_async_copy(filters.at[0], taps.at[pl.ds(4 * cuts, 4)], local_sem.at[3]),
    ]
    for copy in locals_:
        copy.start()
    pl.semaphore_wait(barrier, 19)

    def part(n, source, slot):
        if n == 0:
            return (filters.at[0] if source else taps).at[slot]
        h, q = (n - 1) // 2, (n - 1) % 2
        return (recon.at[0] if source else raw).at[slot, :, pl.ds(512 * q + 128 * h, 128)]

    halo = pltpu.make_async_remote_copy(
        strain, spans.at[0], halo_sem.at[0], halo_sem.at[1],
        device_id=after, device_id_type=MESH,
    )
    halo.start()
    sends, passes = {}, {}
    for n in range(1 + 2 * PIECES):
        for j in range(2):
            mine = 2 * core + j
            sends[n, j] = pltpu.make_async_remote_copy(
                part(n, True, mine), part(n, False, 4 * cuts + mine),
                send_sem.at[j, n], recv_sem.at[j, n],
                device_id=beside[j], device_id_type=MESH,
            )
            sends[n, j].start()
            held = part(n, False, other + mine)
            passes[n, j] = pltpu.make_async_remote_copy(
                held, held, pass_sem.at[j, n], got_sem.at[j, n],
                device_id=partner, device_id_type=MESH,
            )

    def pass_on(parts):
        for n in parts:
            for j in range(2):
                sends[n, j].wait_recv()
                passes[n, j].start()

    locals_[0].wait()
    locals_[1].wait()
    halo.wait()

    lane = lax.broadcasted_iota(jnp.int32, (32, LANES), 1)
    row32 = lax.broadcasted_iota(jnp.int32, (32, LANES), 0)
    low = lane < BLOCK
    known = (row32 >= 16) | (tm > 0)
    first_lane = lax.broadcasted_iota(jnp.int32, (1, LANES), 1)
    none = jnp.zeros((1, LANES), jnp.float32)
    for d in range(2):
        line = jnp.concatenate(
            [spans[r // 16, pl.ds(d, 1), pl.ds(LANES * (r % 16), LANES)] for r in range(32)], axis=0
        )
        for i in range(waves.shape[0]):
            first = offsets[d, i] - (tm - 1) * 2048
            row = first // LANES
            shift = first - row * LANES
            turned = [none] + [
                pltpu.roll(waves[i, pl.ds(d, 1), pl.ds(LANES * r, LANES)], shift, axis=1)
                for r in range(4)
            ] + [none]
            for r in range(5):
                placed = jnp.where(first_lane >= shift, turned[r + 1], turned[r])
                line += jnp.where(row32 == row + r, placed, 0.0)
        line = jnp.where(known, line, 0.0).astype(jnp.bfloat16).astype(jnp.float32)
        swapped = pltpu.roll(line, BLOCK, axis=1)
        if d == 1:
            windows[0] = line
            windows[1] = jnp.where(low, swapped, pltpu.roll(swapped, 31, axis=0))
        else:
            windows[2] = swapped
            windows[3] = jnp.where(low, pltpu.roll(line, 31, axis=0), line)
    half = lax.broadcasted_iota(jnp.int32, (BLOCK, LANES), 1) < BLOCK

    def fill(j, carry):
        for odd in range(2):
            row = j if odd else j + cuts
            tile = 60 + cuts - 2 * j if odd else 61 - cuts - 2 * j
            sides = []
            for kind in (2 + odd, odd):
                wide = jnp.broadcast_to(windows[kind, pl.ds(row, 1), :], (BLOCK, LANES))
                sides.append(pltpu.roll(wide, 0, axis=1, stride=1, stride_axis=0))
            value = jnp.where(half, sides[0], sides[1]).astype(jnp.bfloat16)
            history[pl.ds(pl.multiple_of(tile * BLOCK, BLOCK), BLOCK), :] = value
        return carry

    lax.fori_loop(0, 31, fill, 0)

    select = pair_select(jnp.bfloat16)

    def turn(h, slot):
        pair = jnp.concatenate(
            [raw[slot, :, pl.ds(128 * h, 128)], raw[slot, :, pl.ds(512 + 128 * h, 128)]], axis=1
        )
        turned = lax.dot_general(
            select, pair, (((1,), (1,)), ((), ())), preferred_element_type=jnp.float32
        )
        where = pl.ds(pl.multiple_of(LANES * slot, LANES), LANES)
        weights[h, :, where] = turned.astype(jnp.bfloat16)

    pass_on((0, 1, 2))
    locals_[2].wait()
    locals_[3].wait()
    for h in range(PIECES):
        for i in range(4):
            turn(h, 4 * cuts + i)

    def target_of(k):
        dx, dz = 0, 0
        for i, (a, b) in enumerate(ORDER):
            dx = jnp.where(k == i, a, dx)
            dz = jnp.where(k == i, b, dz)
        return ((x + dx) % 4) * 4 + (z + dz) % 4

    rows = weights.shape[1]

    def piece(k, h):
        lines = pl.ds(h * rows, rows)
        return pltpu.make_async_remote_copy(
            staged.at[k, lines], out.at[bank, lines], out_sem.at[k, h], in_sem.at[k, h],
            device_id={"bank": target_of(k)}, device_id_type=MESH,
        )

    def two_blocks(h, i, carry):
        if h == 0:
            places = [LANES * (15 - target_of(2 * i + b)) for b in range(2)]
            for s in range(8):
                past = jnp.concatenate(
                    [history[pl.ds(pl.multiple_of(p + 256 * s, LANES), 256), :] for p in places],
                    axis=1,
                )
                made = lax.dot_general(
                    taps[s], past, (((0,), (0,)), ((), ())), preferred_element_type=jnp.float32
                )
                basis[i, pl.ds(LANES * s, LANES), :] = made.astype(jnp.bfloat16)
        made = jnp.dot(weights[h], basis[i], preferred_element_type=jnp.float32)
        made = made.astype(jnp.bfloat16)
        for b in range(2):
            staged[2 * i + b, pl.ds(h * rows, rows), :] = made[:, LANES * b:LANES * (b + 1)]
        piece(2 * i, h).start()

        @pl.when(i < 7)
        def _():
            piece(2 * i + 1, h).start()

        if h + 1 < PIECES:
            @pl.when(i == 3)
            def _():
                pass_on((3 + 2 * h, 4 + 2 * h))
        return carry

    for h in range(PIECES):
        for n in ((0, 1, 2) if h == 0 else (1 + 2 * h, 2 + 2 * h)):
            for j in range(2):
                passes[n, j].wait_recv()
        for i in range(4):
            turn(h, other + i)
        lax.fori_loop(0, 8, functools.partial(two_blocks, h), 0)
    own = pltpu.make_async_copy(staged.at[15], out.at[bank], local_sem.at[0])
    own.start()

    def finish(k, carry):
        for h in range(PIECES):
            copy = piece(k, h)
            copy.wait_send()
            copy.wait_recv()
        return carry

    lax.fori_loop(0, 15, finish, 0)
    own.wait()
    for copy in (*sends.values(), *passes.values()):
        copy.wait_send()


def filter_and_exchange(strain, injections, offsets, filters, recon):
    hbm = pl.BlockSpec(memory_space=pltpu.HBM)
    columns = recon.shape[3]
    dma = pltpu.SemaphoreType.DMA
    parts = (2, 1 + 2 * PIECES)
    return pl.pallas_call(
        filter_kernel,
        out_shape=jax.ShapeDtypeStruct((16, columns, LANES), jnp.bfloat16),
        in_specs=[pl.BlockSpec(memory_space=pltpu.SMEM)] + [hbm] * 4,
        out_specs=pl.BlockSpec(memory_space=pl.ANY),
        scratch_shapes=[
            pltpu.VMEM((2, *strain.shape), jnp.float32),
            pltpu.VMEM(injections.shape, jnp.float32),
            pltpu.VMEM((4, 32, LANES), jnp.float32),
            pltpu.VMEM((62 * BLOCK, LANES), jnp.bfloat16),
            pltpu.VMEM((8, 256, 128), jnp.bfloat16),
            pltpu.VMEM((8, 128, columns), jnp.bfloat16),
            pltpu.VMEM((PIECES, columns // PIECES, 1024), jnp.bfloat16),
            pltpu.VMEM((8, 1024, 2 * LANES), jnp.bfloat16),
            pltpu.VMEM((16, columns, LANES), jnp.bfloat16),
            dma((4,)), dma((2,)), dma(parts), dma(parts), dma(parts), dma(parts),
            dma((15, PIECES)), dma((15, PIECES)),
        ],
        compiler_params=pltpu.CompilerParams(
            collective_id=0, has_side_effects=True, vmem_limit_bytes=40 * 2**20
        ),
    )(offsets.T, *(pltpu.with_memory_space_constraint(a, pltpu.HBM) for a in (strain, injections, filters, recon)))


def order_kernel(width, slots, pairs, out, picked):
    base = pl.program_id(0) * width

    def pick(i, carry):
        for u in range(16):
            picked[i * 16 + u] = pairs[slots[base + i * 16 + u]]
        return carry

    lax.fori_loop(0, width // 16, pick, 0)
    select = pair_select(jnp.bfloat16)
    for j in range(width // 256):
        turned = []
        for h in range(2):
            rows = picked.at[pl.ds(j * 256 + h * 128, 128)].reshape(256, LANES)[...]
            turned.append(lax.dot_general(
                rows, select, (((0,), (0,)), ((), ())), preferred_element_type=jnp.float32
            ).astype(jnp.bfloat16))
        stacked = jnp.concatenate(
            [jnp.concatenate([t[:, q * 128:(q + 1) * 128] for t in turned], axis=1) for q in range(2)],
            axis=0,
        )
        mixed = jnp.dot(select, stacked, preferred_element_type=jnp.float32).astype(jnp.bfloat16)
        out[:, :, :, pl.ds(j * 256, 256)] = mixed.reshape(2, BLOCK, 2, 256)


def put_in_order(slot_of, arrived):
    count = slot_of.shape[0]
    width = 1024
    return pl.pallas_call(
        functools.partial(order_kernel, width),
        out_shape=jax.ShapeDtypeStruct((2, BLOCK, 2, count), jnp.bfloat16),
        grid_spec=pltpu.PrefetchScalarGridSpec(
            num_scalar_prefetch=1,
            grid=(count // width,),
            in_specs=[pl.BlockSpec((count, 2, LANES), lambda i, s: (0, 0, 0))],
            out_specs=pl.BlockSpec((2, BLOCK, 2, width), lambda i, s: (0, 0, 0, i)),
            scratch_shapes=[pltpu.VMEM((width, 2, LANES), jnp.bfloat16)],
        ),
        compiler_params=pltpu.CompilerParams(vmem_limit_bytes=40 * 2**20),
    )(slot_of, arrived.reshape(count, 2, LANES))


def per_device(strain, injections, offsets, slot_of, basis_filters, recon_matrix):
    arrived = filter_and_exchange(strain, injections, offsets, basis_filters, recon_matrix)
    return put_in_order(slot_of, arrived)


def solution(mesh):
    return jax.shard_map(
        per_device,
        mesh=mesh,
        in_specs=(
            P(None, "tm"), P(), P(), P(),
            P("bank", "cuts", None, None), P("bank", "cuts", None, None),
        ),
        out_specs=P(None, ("tm", "bank", "cuts"), None, None),
        check_vma=False,
    )
```

time: 102 us -> 88.9 us (0.87)
  Pallas kernels: 94.7 us -> 87.7 us
  local copies, waits for them, and re-layouts: 6.97 us -> 0.69 us
    pallas_call x1, Pallas kernels: 76.3 us -> 70.8 us  [filter_and_exchange(): pl.pallas_call(filter_kernel, out_shape=jax.ShapeDtypeStruct((16, columns...]
    unnamed x10 -> x4, local copies, waits for them, and re-layouts: 5.56 us -> 0.69 us
    pallas_call x1 -> x0, Pallas kernels: 1.58 us -> none  [inject(): pl.pallas_call(inject_kernel, out_shape=jax.ShapeDtypeStruct(shaped.shape...]
    reshape x1 -> x0, local copies, waits for them, and re-layouts: 1.4 us -> none  [inject(): waves = injections.reshape(*injections.shape[:2], -1, LANES)]
where the time goes in v2:
time: 88.9 us; the launch traced here: 88.4 us
  Pallas kernels  87.7 us (99%)
    pallas_call x1, Pallas kernels, filter_and_exchange(): pl.pallas_call(filter_kernel, out_shape=jax.ShapeDtypeStruct((16, columns...  70.8 us
    pallas_call x1, Pallas kernels, put_in_order(): pl.pallas_call(functools.partial(order_kernel, width), out_shape=jax.Shap...  16.9 us

profile of v2, /device:TPU:1, one launch (start us, length us, event | category | flops | bytes accessed | tf_op | source)
XLA Modules:
  0.0 88.4 jit_solution(17139455473504003000)
XLA Ops:
  0.0 0.0 copy-start
  0.0 0.0 copy-start.1
  0.0 0.7 copy-done.1
  0.7 70.8 %shard_map.64 = bf16[16,1024,128]{2,1,0:T(8,128)(2,1)S(1)} custom-call(s32[2,8]{1,0:T(2,128)S(1)} %bitcast.3, f32[2,2048]{1,0:T(2,128)} %strain.1, f32[8,2,512]{2,1,0:T(2,128)} %injections.1, bf16[1,4,256,128]{3,2,1,0:T(8,128)(2,1)} %filters.1, bf16[1,4,128,1024]{3,2,1,0:T(8,128)(2,1)} %recon.1), custom_call_target="tpu_custom_call" | custom-call | tf_op jit(solution)/shard_map/pallas_call | solution.py:228
  71.5 0.0 copy-done
  71.6 16.9 %shard_map.65 = bf16[2,64,2,8192]{3,2,1,0:T(2,128)(2,1)} custom-call(s32[8192]{0:T(1024)S(1)} %copy-done, bf16[8192,2,128]{2,1,0:T(2,128)(2,1)S(1)} %bitcast.2), custom_call_target="tpu_custom_call" | custom-call | tf_op jit(solution)/shard_map/pallas_call | solution.py:280
Async XLA Ops:
  0.0 71.5 %copy-start = (s32[8192]{0:T(1024)S(1)}, s32[8192]{0:T(1024)}, u32[]{:S(2)}) copy-start(s32[8192]{0:T(1024)} %slots.1) | copy-start | bytes 98308
  0.0 0.7 copy-start.1

commit v3 on v2

--- a/solution.py
+++ b/solution.py
@@ -12,10 +12,10 @@
 BLOCK = 64
 PIECES = 4
 ORDER = (
+    (2, 1), (2, 3), (1, 2), (3, 2),
+    (2, 2), (2, 0), (0, 2),
     (1, 1), (3, 3), (1, 3), (3, 1),
     (1, 0), (3, 0), (0, 1), (0, 3),
-    (2, 2), (2, 0), (0, 2),
-    (2, 1), (2, 3), (1, 2), (3, 2),
 )
 
 
@@ -249,46 +249,91 @@
     )(offsets.T, *(pltpu.with_memory_space_constraint(a, pltpu.HBM) for a in (strain, injections, filters, recon)))
 
 
-def order_kernel(width, slots, pairs, out, picked):
-    base = pl.program_id(0) * width
-
-    def pick(i, carry):
-        for u in range(16):
-            picked[i * 16 + u] = pairs[slots[base + i * 16 + u]]
+def pick_kernel(slots, pairs, out, even, odd, sem):
+    width = even.shape[0]
+    count = slots.shape[0] // width
+    held = (even, odd)
+
+    def fetch(c, b):
+        lines = pl.ds(pl.multiple_of(c * width, width), width)
+        return pltpu.make_async_copy(slots.at[lines], held[b], sem.at[b])
+
+    for b in range(2):
+        fetch(b, b).start()
+
+    def step(i, carry):
+        for b in range(2):
+            c = 2 * i + b
+            fetch(c, b).wait()
+            base = c * width
+            for u in range(width):
+                out[base + u] = pairs[held[b][u]]
+
+            @pl.when(c + 2 < count)
+            def _():
+                fetch(c + 2, b).start()
         return carry
 
-    lax.fori_loop(0, width // 16, pick, 0)
-    select = pair_select(jnp.bfloat16)
-    for j in range(width // 256):
-        turned = []
-        for h in range(2):
-            rows = picked.at[pl.ds(j * 256 + h * 128, 128)].reshape(256, LANES)[...]
-            turned.append(lax.dot_general(
-                rows, select, (((0,), (0,)), ((), ())), preferred_element_type=jnp.float32
+    lax.fori_loop(0, count // 2, step, 0)
+
+
+def turn_kernel(picked, out, select, spread):
+    @pl.when(pl.program_id(0) == 0)
+    def _():
+        select[...] = pair_select(jnp.bfloat16)
+        row = lax.broadcasted_iota(jnp.int32, (256, 256), 0)
+        col = lax.broadcasted_iota(jnp.int32, (256, 256), 1)
+        spread[...] = ((row // 16 == col % 16) & (row % 16 == col // 16)).astype(jnp.bfloat16)
+
+    for g in range(picked.shape[0] // 2048):
+        tiles = []
+        for j in range(8):
+            tiles.append(lax.dot_general(
+                picked[pl.ds((8 * g + j) * 256, 256), :], select[...], (((0,), (0,)), ((), ())),
+                preferred_element_type=jnp.float32,
             ).astype(jnp.bfloat16))
-        stacked = jnp.concatenate(
-            [jnp.concatenate([t[:, q * 128:(q + 1) * 128] for t in turned], axis=1) for q in range(2)],
-            axis=0,
-        )
-        mixed = jnp.dot(select, stacked, preferred_element_type=jnp.float32).astype(jnp.bfloat16)
-        out[:, :, :, pl.ds(j * 256, 256)] = mixed.reshape(2, BLOCK, 2, 256)
+        for t in range(0, 8, 2):
+            sides = [
+                jnp.concatenate(
+                    [tiles[j][16 * u:16 * u + 16, 128 * q:128 * q + 128]
+                     for j in range(8) for q in range(2)],
+                    axis=0,
+                )
+                for u in (t, t + 1)
+            ]
+            mixed = jnp.dot(
+                spread[...], jnp.concatenate(sides, axis=1), preferred_element_type=jnp.float32
+            ).astype(jnp.bfloat16)
+            for h in range(2):
+                out[pl.ds(16 * (t + h), 16), pl.ds(16 * g, 16), :] = (
+                    mixed[:, 128 * h:128 * h + 128].reshape(16, 16, LANES)
+                )
 
 
 def put_in_order(slot_of, arrived):
     count = slot_of.shape[0]
-    width = 1024
-    return pl.pallas_call(
-        functools.partial(order_kernel, width),
-        out_shape=jax.ShapeDtypeStruct((2, BLOCK, 2, count), jnp.bfloat16),
-        grid_spec=pltpu.PrefetchScalarGridSpec(
-            num_scalar_prefetch=1,
-            grid=(count // width,),
-            in_specs=[pl.BlockSpec((count, 2, LANES), lambda i, s: (0, 0, 0))],
-            out_specs=pl.BlockSpec((2, BLOCK, 2, width), lambda i, s: (0, 0, 0, i)),
-            scratch_shapes=[pltpu.VMEM((width, 2, LANES), jnp.bfloat16)],
-        ),
+    width, step = 1024, 2048
+    vmem = pl.BlockSpec(memory_space=pltpu.VMEM)
+    picked = pl.pallas_call(
+        pick_kernel,
+        out_shape=jax.ShapeDtypeStruct((count, 2, LANES), jnp.bfloat16),
+        in_specs=[pl.BlockSpec(memory_space=pl.ANY), vmem],
+        out_specs=vmem,
+        scratch_shapes=[pltpu.SMEM((width,), jnp.int32)] * 2 + [pltpu.SemaphoreType.DMA((2,))],
         compiler_params=pltpu.CompilerParams(vmem_limit_bytes=40 * 2**20),
     )(slot_of, arrived.reshape(count, 2, LANES))
+    tiles = count // LANES
+    turned = pl.pallas_call(
+        turn_kernel,
+        out_shape=jax.ShapeDtypeStruct((2 * BLOCK, 2 * tiles, LANES), jnp.bfloat16),
+        grid=(count // step,),
+        in_specs=[pl.BlockSpec((2 * step, LANES), lambda i: (i, 0))],
+        out_specs=pl.BlockSpec((2 * BLOCK, step // BLOCK, LANES), lambda i: (0, i, 0)),
+        scratch_shapes=[pltpu.VMEM((256, 256), jnp.bfloat16)] * 2,
+        compiler_params=pltpu.CompilerParams(vmem_limit_bytes=40 * 2**20),
+    )(picked.reshape(2 * count, LANES))
+    turned = turned.reshape(2 * BLOCK, tiles, 2, LANES).transpose(0, 2, 1, 3)
+    return turned.reshape(2, BLOCK, 2, count)
 
 
 def per_device(strain, injections, offsets, slot_of, basis_filters, recon_matrix):

time: 88.9 us -> 80.9 us (0.910)
  Pallas kernels: 87.7 us -> 79.3 us
    pallas_call x1 -> x2, Pallas kernels: 16.9 us -> 10.3 us  [the longest x1 5.18 us: put_in_order(): pl.pallas_call(turn_kernel, out_shape=jax.ShapeDtypeStruct((2 * BLOCK, 2...]
    pallas_call x1, Pallas kernels: 70.8 us -> 69 us  [filter_and_exchange(): pl.pallas_call(filter_kernel, out_shape=jax.ShapeDtypeStruct((16, columns...]
where the time goes in v3:
time: 80.9 us; the launch traced here: 80 us
  Pallas kernels  79.3 us (98%)
    pallas_call x1, Pallas kernels, filter_and_exchange(): pl.pallas_call(filter_kernel, out_shape=jax.ShapeDtypeStruct((16, columns...  69 us
    pallas_call x1, Pallas kernels, put_in_order(): pl.pallas_call(turn_kernel, out_shape=jax.ShapeDtypeStruct((2 * BLOCK, 2...  5.18 us
    pallas_call x1, Pallas kernels, put_in_order(): pl.pallas_call(pick_kernel, out_shape=jax.ShapeDtypeStruct((count, 2, LAN...  5.13 us

profile of v3, /device:TPU:1, one launch (start us, length us, event | category | flops | bytes accessed | tf_op | source)
XLA Modules:
  0.0 80.0 jit_solution(3382155145831125485)
XLA Ops:
  0.0 0.0 copy-start
  0.0 0.0 copy-start.1
  0.0 0.7 copy-done.1
  0.7 69.0 %shard_map.64 = bf16[16,1024,128]{2,1,0:T(8,128)(2,1)S(1)} custom-call(s32[2,8]{1,0:T(2,128)S(1)} %bitcast.10, f32[2,2048]{1,0:T(2,128)} %strain.1, f32[8,2,512]{2,1,0:T(2,128)} %injections.1, bf16[1,4,256,128]{3,2,1,0:T(8,128)(2,1)} %filters.1, bf16[1,4,128,1024]{3,2,1,0:T(8,128)(2,1)} %recon.1), custom_call_target="tpu_custom_call" | custom-call | tf_op jit(solution)/shard_map/pallas_call | solution.py:228
  69.7 0.0 copy-done
  69.7 5.1 %shard_map.65 = bf16[8192,2,128]{2,1,0:T(2,128)(2,1)S(1)} custom-call(s32[8192]{0:T(1024)S(1)} %copy-done, bf16[8192,2,128]{2,1,0:T(2,128)(2,1)S(1)} %bitcast.9), custom_call_target="tpu_custom_call" | custom-call | tf_op jit(solution)/shard_map/pallas_call | solution.py:317
  74.9 5.2 %shard_map.66 = bf16[128,128,128]{2,1,0:T(8,128)(2,1)} custom-call(bf16[16384,128]{1,0:T(8,128)(2,1)S(1)} %bitcast.8), custom_call_target="tpu_custom_call" | custom-call | tf_op jit(solution)/shard_map/pallas_call | solution.py:326
Async XLA Ops:
  0.0 69.7 %copy-start = (s32[8192]{0:T(1024)S(1)}, s32[8192]{0:T(1024)}, u32[]{:S(2)}) copy-start(s32[8192]{0:T(1024)} %slots.1) | copy-start | bytes 98308
  0.0 0.7 copy-start.1

commit v4 on v3

--- a/solution.py
+++ b/solution.py
@@ -11,6 +11,7 @@
 LANES = 128
 BLOCK = 64
 PIECES = 4
+EARLY = 1
 ORDER = (
     (2, 1), (2, 3), (1, 2), (3, 2),
     (2, 2), (2, 0), (0, 2),
@@ -27,7 +28,7 @@
 
 def filter_kernel(
     offsets, strain, injections, filters, recon, out,
-    spans, waves, windows, history, taps, raw, weights, basis, staged,
+    places, spans, waves, windows, history, taps, raw, weights, basis, staged,
     local_sem, halo_sem, send_sem, recv_sem, pass_sem, got_sem, out_sem, in_sem,
 ):
     tm, bank, cuts = lax.axis_index("tm"), lax.axis_index("bank"), lax.axis_index("cuts")
@@ -47,6 +48,7 @@
         pltpu.make_async_copy(injections, waves, local_sem.at[1]),
         pltpu.make_async_copy(recon.at[0], raw.at[pl.ds(4 * cuts, 4)], local_sem.at[2]),
         pltpu.make_async_copy(filters.at[0], taps.at[pl.ds(4 * cuts, 4)], local_sem.at[3]),
+        pltpu.make_async_copy(offsets, places, local_sem.at[4]),
     ]
     for copy in locals_:
         copy.start()
@@ -87,6 +89,7 @@
 
     locals_[0].wait()
     locals_[1].wait()
+    locals_[4].wait()
     halo.wait()
 
     lane = lax.broadcasted_iota(jnp.int32, (32, LANES), 1)
@@ -100,7 +103,7 @@
             [spans[r // 16, pl.ds(d, 1), pl.ds(LANES * (r % 16), LANES)] for r in range(32)], axis=0
         )
         for i in range(waves.shape[0]):
-            first = offsets[d, i] - (tm - 1) * 2048
+            first = places[d, i] - (tm - 1) * 2048
             row = first // LANES
             shift = first - row * LANES
             turned = [none] + [
@@ -146,13 +149,6 @@
         where = pl.ds(pl.multiple_of(LANES * slot, LANES), LANES)
         weights[h, :, where] = turned.astype(jnp.bfloat16)
 
-    pass_on((0, 1, 2))
-    locals_[2].wait()
-    locals_[3].wait()
-    for h in range(PIECES):
-        for i in range(4):
-            turn(h, 4 * cuts + i)
-
     def target_of(k):
         dx, dz = 0, 0
         for i, (a, b) in enumerate(ORDER):
@@ -169,18 +165,27 @@
             device_id={"bank": target_of(k)}, device_id_type=MESH,
         )
 
+    def make_basis(i):
+        starts = [LANES * (15 - target_of(2 * i + b)) for b in range(2)]
+        for s in range(8):
+            past = jnp.concatenate(
+                [history[pl.ds(pl.multiple_of(p + 256 * s, LANES), 256), :] for p in starts],
+                axis=1,
+            )
+            made = lax.dot_general(
+                taps[s], past, (((0,), (0,)), ((), ())), preferred_element_type=jnp.float32
+            )
+            basis[i, pl.ds(LANES * s, LANES), :] = made.astype(jnp.bfloat16)
+
+    def early(i, carry):
+        make_basis(i)
+        return carry
+
     def two_blocks(h, i, carry):
         if h == 0:
-            places = [LANES * (15 - target_of(2 * i + b)) for b in range(2)]
-            for s in range(8):
-                past = jnp.concatenate(
-                    [history[pl.ds(pl.multiple_of(p + 256 * s, LANES), 256), :] for p in places],
-                    axis=1,
-                )
-                made = lax.dot_general(
-                    taps[s], past, (((0,), (0,)), ((), ())), preferred_element_type=jnp.float32
-                )
-                basis[i, pl.ds(LANES * s, LANES), :] = made.astype(jnp.bfloat16)
+            @pl.when(i >= EARLY)
+            def _():
+                make_basis(i)
         made = jnp.dot(weights[h], basis[i], preferred_element_type=jnp.float32)
         made = made.astype(jnp.bfloat16)
         for b in range(2):
@@ -197,12 +202,27 @@
                 pass_on((3 + 2 * h, 4 + 2 * h))
         return carry
 
+    pass_on((0,))
+    locals_[2].wait()
+    locals_[3].wait()
+    for i in range(4):
+        turn(0, 4 * cuts + i)
+    for j in range(2):
+        passes[0, j].wait_recv()
+    lax.fori_loop(0, EARLY, early, 0)
+    pass_on((1, 2))
+    for i in range(2):
+        turn(0, other + 2 * core + i)
     for h in range(PIECES):
-        for n in ((0, 1, 2) if h == 0 else (1 + 2 * h, 2 + 2 * h)):
+        for n in (1 + 2 * h, 2 + 2 * h):
             for j in range(2):
                 passes[n, j].wait_recv()
-        for i in range(4):
-            turn(h, other + i)
+        if h == 0:
+            for i in range(2):
+                turn(0, other + 2 * (1 - core) + i)
+        else:
+            for i in range(8):
+                turn(h, i)
         lax.fori_loop(0, 8, functools.partial(two_blocks, h), 0)
     own = pltpu.make_async_copy(staged.at[15], out.at[bank], local_sem.at[0])
     own.start()
@@ -228,9 +248,10 @@
     return pl.pallas_call(
         filter_kernel,
         out_shape=jax.ShapeDtypeStruct((16, columns, LANES), jnp.bfloat16),
-        in_specs=[pl.BlockSpec(memory_space=pltpu.SMEM)] + [hbm] * 4,
+        in_specs=[hbm] * 5,
         out_specs=pl.BlockSpec(memory_space=pl.ANY),
         scratch_shapes=[
+            pltpu.SMEM(offsets.shape[::-1], jnp.int32),
             pltpu.VMEM((2, *strain.shape), jnp.float32),
             pltpu.VMEM(injections.shape, jnp.float32),
             pltpu.VMEM((4, 32, LANES), jnp.float32),
@@ -240,13 +261,16 @@
             pltpu.VMEM((PIECES, columns // PIECES, 1024), jnp.bfloat16),
             pltpu.VMEM((8, 1024, 2 * LANES), jnp.bfloat16),
             pltpu.VMEM((16, columns, LANES), jnp.bfloat16),
-            dma((4,)), dma((2,)), dma(parts), dma(parts), dma(parts), dma(parts),
+            dma((5,)), dma((2,)), dma(parts), dma(parts), dma(parts), dma(parts),
             dma((15, PIECES)), dma((15, PIECES)),
         ],
         compiler_params=pltpu.CompilerParams(
             collective_id=0, has_side_effects=True, vmem_limit_bytes=40 * 2**20
         ),
-    )(offsets.T, *(pltpu.with_memory_space_constraint(a, pltpu.HBM) for a in (strain, injections, filters, recon)))
+    )(*(
+        pltpu.with_memory_space_constraint(a, pltpu.HBM)
+        for a in (offsets.T, strain, injections, filters, recon)
+    ))
 
 
 def pick_kernel(slots, pairs, out, even, odd, sem):

time: 80.9 us -> 77.6 us (0.959)
  Pallas kernels: 79.3 us -> 77.5 us
    pallas_call x1, Pallas kernels: 69 us -> 67.2 us  [filter_and_exchange(): pl.pallas_call(filter_kernel, out_shape=jax.ShapeDtypeStruct((16, columns...]
where the time goes in v4:
time: 77.6 us; the launch traced here: 77.5 us
  Pallas kernels  77.5 us (100%)
    pallas_call x1, Pallas kernels, filter_and_exchange(): pl.pallas_call(filter_kernel, out_shape=jax.ShapeDtypeStruct((16, columns...  67.2 us
    pallas_call x1, Pallas kernels, put_in_order(): pl.pallas_call(turn_kernel, out_shape=jax.ShapeDtypeStruct((2 * BLOCK, 2...  5.18 us
    pallas_call x1, Pallas kernels, put_in_order(): pl.pallas_call(pick_kernel, out_shape=jax.ShapeDtypeStruct((count, 2, LAN...  5.13 us

profile of v4, /device:TPU:1, one launch (start us, length us, event | category | flops | bytes accessed | tf_op | source)
XLA Modules:
  0.0 77.5 jit_solution(17417125699356078538)
XLA Ops:
  0.0 0.0 copy-start
  0.0 67.2 %shard_map.64 = bf16[16,1024,128]{2,1,0:T(8,128)(2,1)S(1)} custom-call(s32[2,8]{1,0:T(2,128)} %bitcast.10, f32[2,2048]{1,0:T(2,128)} %strain.1, f32[8,2,512]{2,1,0:T(2,128)} %injections.1, bf16[1,4,256,128]{3,2,1,0:T(8,128)(2,1)} %filters.1, bf16[1,4,128,1024]{3,2,1,0:T(8,128)(2,1)} %recon.1), custom_call_target="tpu_custom_call" | custom-call | tf_op jit(solution)/shard_map/pallas_call | solution.py:248
  67.2 0.0 copy-done
  67.2 5.1 %shard_map.65 = bf16[8192,2,128]{2,1,0:T(2,128)(2,1)S(1)} custom-call(s32[8192]{0:T(1024)S(1)} %copy-done, bf16[8192,2,128]{2,1,0:T(2,128)(2,1)S(1)} %bitcast.9), custom_call_target="tpu_custom_call" | custom-call | tf_op jit(solution)/shard_map/pallas_call | solution.py:341
  72.4 5.2 %shard_map.66 = bf16[128,128,128]{2,1,0:T(8,128)(2,1)} custom-call(bf16[16384,128]{1,0:T(8,128)(2,1)S(1)} %bitcast.8), custom_call_target="tpu_custom_call" | custom-call | tf_op jit(solution)/shard_map/pallas_call | solution.py:350
Async XLA Ops:
  0.0 67.2 %copy-start = (s32[8192]{0:T(1024)S(1)}, s32[8192]{0:T(1024)}, u32[]{:S(2)}) copy-start(s32[8192]{0:T(1024)} %slots.1) | copy-start | bytes 98308

commit v5 on v4

--- a/solution.py
+++ b/solution.py
@@ -135,7 +135,8 @@
             history[pl.ds(pl.multiple_of(tile * BLOCK, BLOCK), BLOCK), :] = value
         return carry
 
-    lax.fori_loop(0, 31, fill, 0)
+    for j in range(31):
+        fill(j, 0)
 
     select = pair_select(jnp.bfloat16)
 
@@ -309,34 +310,45 @@
         col = lax.broadcasted_iota(jnp.int32, (256, 256), 1)
         spread[...] = ((row // 16 == col % 16) & (row % 16 == col // 16)).astype(jnp.bfloat16)
 
-    for g in range(picked.shape[0] // 2048):
-        tiles = []
-        for j in range(8):
-            tiles.append(lax.dot_general(
-                picked[pl.ds((8 * g + j) * 256, 256), :], select[...], (((0,), (0,)), ((), ())),
-                preferred_element_type=jnp.float32,
-            ).astype(jnp.bfloat16))
+    def tile(g, j):
+        return lax.dot_general(
+            picked[pl.ds((8 * g + j) * 256, 256), :], select[...], (((0,), (0,)), ((), ())),
+            preferred_element_type=jnp.float32,
+        ).astype(jnp.bfloat16)
+
+    def finish(g, tiles, t):
+        sides = [
+            jnp.concatenate(
+                [tiles[j][16 * u:16 * u + 16, 128 * q:128 * q + 128]
+                 for j in range(8) for q in range(2)],
+                axis=0,
+            )
+            for u in (t, t + 1)
+        ]
+        mixed = jnp.dot(
+            spread[...], jnp.concatenate(sides, axis=1), preferred_element_type=jnp.float32
+        ).astype(jnp.bfloat16)
+        for h in range(2):
+            out[pl.ds(16 * (t + h), 16), pl.ds(16 * g, 16), :] = (
+                mixed[:, 128 * h:128 * h + 128].reshape(16, 16, LANES)
+            )
+
+    groups = picked.shape[0] // 2048
+    tiles = [tile(0, j) for j in range(8)]
+    for g in range(groups):
+        later = []
         for t in range(0, 8, 2):
-            sides = [
-                jnp.concatenate(
-                    [tiles[j][16 * u:16 * u + 16, 128 * q:128 * q + 128]
-                     for j in range(8) for q in range(2)],
-                    axis=0,
-                )
-                for u in (t, t + 1)
-            ]
-            mixed = jnp.dot(
-                spread[...], jnp.concatenate(sides, axis=1), preferred_element_type=jnp.float32
-            ).astype(jnp.bfloat16)
-            for h in range(2):
-                out[pl.ds(16 * (t + h), 16), pl.ds(16 * g, 16), :] = (
-                    mixed[:, 128 * h:128 * h + 128].reshape(16, 16, LANES)
-                )
+            if g + 1 < groups:
+                later.append(tile(g + 1, t))
+            finish(g, tiles, t)
+            if g + 1 < groups:
+                later.append(tile(g + 1, t + 1))
+        tiles = later
 
 
 def put_in_order(slot_of, arrived):
     count = slot_of.shape[0]
-    width, step = 1024, 2048
+    width, step = 1024, 4096
     vmem = pl.BlockSpec(memory_space=pltpu.VMEM)
     picked = pl.pallas_call(
         pick_kernel,

time: 77.6 us -> 76.6 us (0.987)
  Pallas kernels: 77.5 us -> 76.5 us
    pallas_call x1, Pallas kernels: 5.18 us -> 4.26 us  [put_in_order(): pl.pallas_call(turn_kernel, out_shape=jax.ShapeDtypeStruct((2 * BLOCK, 2...]
where the time goes in v5:
time: 76.6 us
  Pallas kernels  76.5 us (100%)
    pallas_call x1, Pallas kernels, filter_and_exchange(): pl.pallas_call(filter_kernel, out_shape=jax.ShapeDtypeStruct((16, columns...  67.1 us
    pallas_call x1, Pallas kernels, put_in_order(): pl.pallas_call(pick_kernel, out_shape=jax.ShapeDtypeStruct((count, 2, LAN...  5.13 us
    pallas_call x1, Pallas kernels, put_in_order(): pl.pallas_call(turn_kernel, out_shape=jax.ShapeDtypeStruct((2 * BLOCK, 2...  4.26 us

profile of v5, /device:TPU:1, one launch (start us, length us, event | category | flops | bytes accessed | tf_op | source)
XLA Modules:
  0.0 76.6 jit_solution(10427928433633104298)
XLA Ops:
  0.0 0.0 copy-start
  0.0 67.1 %shard_map.64 = bf16[16,1024,128]{2,1,0:T(8,128)(2,1)S(1)} custom-call(s32[2,8]{1,0:T(2,128)} %bitcast.10, f32[2,2048]{1,0:T(2,128)} %strain.1, f32[8,2,512]{2,1,0:T(2,128)} %injections.1, bf16[1,4,256,128]{3,2,1,0:T(8,128)(2,1)} %filters.1, bf16[1,4,128,1024]{3,2,1,0:T(8,128)(2,1)} %recon.1), custom_call_target="tpu_custom_call" | custom-call | tf_op jit(solution)/shard_map/pallas_call | solution.py:249
  67.1 0.0 copy-done
  67.2 5.1 %shard_map.65 = bf16[8192,2,128]{2,1,0:T(2,128)(2,1)S(1)} custom-call(s32[8192]{0:T(1024)S(1)} %copy-done, bf16[8192,2,128]{2,1,0:T(2,128)(2,1)S(1)} %bitcast.9), custom_call_target="tpu_custom_call" | custom-call | tf_op jit(solution)/shard_map/pallas_call | solution.py:353
  72.3 4.3 %shard_map.66 = bf16[128,128,128]{2,1,0:T(8,128)(2,1)} custom-call(bf16[16384,128]{1,0:T(8,128)(2,1)S(1)} %bitcast.8), custom_call_target="tpu_custom_call" | custom-call | tf_op jit(solution)/shard_map/pallas_call | solution.py:362
Async XLA Ops:
  0.0 67.1 %copy-start = (s32[8192]{0:T(1024)S(1)}, s32[8192]{0:T(1024)}, u32[]{:S(2)}) copy-start(s32[8192]{0:T(1024)} %slots.1) | copy-start | bytes 98308

commit v6 on v5

--- a/solution.py
+++ b/solution.py
@@ -155,6 +155,7 @@
         for i, (a, b) in enumerate(ORDER):
             dx = jnp.where(k == i, a, dx)
             dz = jnp.where(k == i, b, dz)
+        dx, dz = jnp.where(core == 1, dz, dx), jnp.where(core == 1, dx, dz)
         return ((x + dx) % 4) * 4 + (z + dz) % 4
 
     rows = weights.shape[1]

time: 76.6 us -> 75.8 us (0.990)
  Pallas kernels: 76.5 us -> 75.4 us
    pallas_call x1, Pallas kernels: 67.1 us -> 66 us  [filter_and_exchange(): pl.pallas_call(filter_kernel, out_shape=jax.ShapeDtypeStruct((16, columns...]
where the time goes in v6:
time: 75.8 us; the launch traced here: 75.4 us
  Pallas kernels  75.4 us (99%)
    pallas_call x1, Pallas kernels, filter_and_exchange(): pl.pallas_call(filter_kernel, out_shape=jax.ShapeDtypeStruct((16, columns...  66 us
    pallas_call x1, Pallas kernels, put_in_order(): pl.pallas_call(pick_kernel, out_shape=jax.ShapeDtypeStruct((count, 2, LAN...  5.13 us
    pallas_call x1, Pallas kernels, put_in_order(): pl.pallas_call(turn_kernel, out_shape=jax.ShapeDtypeStruct((2 * BLOCK, 2...  4.26 us

profile of v6, /device:TPU:1, one launch (start us, length us, event | category | flops | bytes accessed | tf_op | source)
XLA Modules:
  0.0 75.4 jit_solution(11798284052171612476)
XLA Ops:
  0.0 0.0 copy-start
  0.0 66.0 %shard_map.64 = bf16[16,1024,128]{2,1,0:T(8,128)(2,1)S(1)} custom-call(s32[2,8]{1,0:T(2,128)} %bitcast.10, f32[2,2048]{1,0:T(2,128)} %strain.1, f32[8,2,512]{2,1,0:T(2,128)} %injections.1, bf16[1,4,256,128]{3,2,1,0:T(8,128)(2,1)} %filters.1, bf16[1,4,128,1024]{3,2,1,0:T(8,128)(2,1)} %recon.1), custom_call_target="tpu_custom_call" | custom-call | tf_op jit(solution)/shard_map/pallas_call | solution.py:250
  66.0 0.0 copy-done
  66.0 5.1 %shard_map.65 = bf16[8192,2,128]{2,1,0:T(2,128)(2,1)S(1)} custom-call(s32[8192]{0:T(1024)S(1)} %copy-done, bf16[8192,2,128]{2,1,0:T(2,128)(2,1)S(1)} %bitcast.9), custom_call_target="tpu_custom_call" | custom-call | tf_op jit(solution)/shard_map/pallas_call | solution.py:354
  71.2 4.3 %shard_map.66 = bf16[128,128,128]{2,1,0:T(8,128)(2,1)} custom-call(bf16[16384,128]{1,0:T(8,128)(2,1)S(1)} %bitcast.8), custom_call_target="tpu_custom_call" | custom-call | tf_op jit(solution)/shard_map/pallas_call | solution.py:363
Async XLA Ops:
  0.0 66.0 %copy-start = (s32[8192]{0:T(1024)S(1)}, s32[8192]{0:T(1024)}, u32[]{:S(2)}) copy-start(s32[8192]{0:T(1024)} %slots.1) | copy-start | bytes 98308

commit v7 on v6

--- a/solution.py
+++ b/solution.py
@@ -211,8 +211,8 @@
         turn(0, 4 * cuts + i)
     for j in range(2):
         passes[0, j].wait_recv()
+    pass_on((1, 2))
     lax.fori_loop(0, EARLY, early, 0)
-    pass_on((1, 2))
     for i in range(2):
         turn(0, other + 2 * core + i)
     for h in range(PIECES):

time: 75.8 us -> 75.5 us (level)
  no operation moved by 1% of the time
where the time goes in v7:
time: 75.5 us; the launch traced here: 75.4 us
  Pallas kernels  75.4 us (100%)
    pallas_call x1, Pallas kernels, filter_and_exchange(): pl.pallas_call(filter_kernel, out_shape=jax.ShapeDtypeStruct((16, columns...  66 us
    pallas_call x1, Pallas kernels, put_in_order(): pl.pallas_call(pick_kernel, out_shape=jax.ShapeDtypeStruct((count, 2, LAN...  5.13 us
    pallas_call x1, Pallas kernels, put_in_order(): pl.pallas_call(turn_kernel, out_shape=jax.ShapeDtypeStruct((2 * BLOCK, 2...  4.26 us

profile of v7, /device:TPU:1, one launch (start us, length us, event | category | flops | bytes accessed | tf_op | source)
XLA Modules:
  0.0 75.4 jit_solution(4344995936820774638)
XLA Ops:
  0.0 0.0 copy-start
  0.0 66.0 %shard_map.64 = bf16[16,1024,128]{2,1,0:T(8,128)(2,1)S(1)} custom-call(s32[2,8]{1,0:T(2,128)} %bitcast.10, f32[2,2048]{1,0:T(2,128)} %strain.1, f32[8,2,512]{2,1,0:T(2,128)} %injections.1, bf16[1,4,256,128]{3,2,1,0:T(8,128)(2,1)} %filters.1, bf16[1,4,128,1024]{3,2,1,0:T(8,128)(2,1)} %recon.1), custom_call_target="tpu_custom_call" | custom-call | tf_op jit(solution)/shard_map/pallas_call | solution.py:250
  66.0 0.0 copy-done
  66.0 5.1 %shard_map.65 = bf16[8192,2,128]{2,1,0:T(2,128)(2,1)S(1)} custom-call(s32[8192]{0:T(1024)S(1)} %copy-done, bf16[8192,2,128]{2,1,0:T(2,128)(2,1)S(1)} %bitcast.9), custom_call_target="tpu_custom_call" | custom-call | tf_op jit(solution)/shard_map/pallas_call | solution.py:354
  71.2 4.3 %shard_map.66 = bf16[128,128,128]{2,1,0:T(8,128)(2,1)} custom-call(bf16[16384,128]{1,0:T(8,128)(2,1)S(1)} %bitcast.8), custom_call_target="tpu_custom_call" | custom-call | tf_op jit(solution)/shard_map/pallas_call | solution.py:363
Async XLA Ops:
  0.0 66.0 %copy-start = (s32[8192]{0:T(1024)S(1)}, s32[8192]{0:T(1024)}, u32[]{:S(2)}) copy-start(s32[8192]{0:T(1024)} %slots.1) | copy-start | bytes 98308
